TPU v7x, 32 devices: a whole 2x2x4 slice. The times are simulated.
32 devices in a mesh: row: 2 (over y), col: 16 (over z, x, core).
Axes of the slice: x: 2, y: 2, z: 4, core: 2. Of those that a mesh axis runs over, the one named last changes fastest.
Arguments:
- object_field: float32 [2, 512, 4096], P(None, 'row', 'col'), may hold values from -6 to 6
- probe_field: float32 [2, 256, 256], replicated, may hold values from -4.2 to 4.2
- amplitudes: bfloat16 [2, 16, 6, 256, 256], P('row', 'col'), may hold values from 0 to 2
- offsets: int32 [2, 16, 6, 2], P('row', 'col'), may hold values from 0 to 256
- counts: int32 [2, 16], P('row', 'col'), may hold values from 2 to 6
Outputs:
- updated_object: float32 [2, 512, 4096], P(None, 'row', 'col')
Inputs may be any that keep to these rules, and one draw needn't show every extreme that they name: Tile (r, c) uses slots 0 to counts[r, c] - 1; offsets and amplitudes of the other slots are ignored.
All inputs are finite; a program needn't handle non-finite values.
Results may differ from a plain program's by a relative error of at most 0.0021.
Values sent between devices are 32-bit elements; how exact they have to be, the bound alone decides.
A program may use at most 64 MiB of HBM per device.

v0:
```python
import functools
import math

import jax
import jax.numpy as jnp
import numpy as np
from jax import lax
from jax.experimental import pallas as pl
from jax.experimental.pallas import tpu as pltpu
from jax.sharding import PartitionSpec as P

TILE = 256
RIM = 128
MAXPOS = 6
ITERS = 2
LANES = 128
CHUNK = 64

smooth_term = 0.25
step_size = 0.5
regular_term = 1.0

AXES = ("row", "col")
SIDES = [(-1, 0), (1, 0), (0, -1), (0, 1), (-1, -1), (-1, 1), (1, -1), (1, 1)]


def dft_tables():
    positions = np.arange(TILE)
    phase_step = (positions[:, None] * positions[None, :]) % TILE
    angle = phase_step.astype(np.float32) * np.float32(2.0 * math.pi / TILE)
    scale = np.float32(1.0 / math.sqrt(TILE))
    real = np.cos(angle).astype(np.float32) * scale
    imag = -np.sin(angle).astype(np.float32) * scale
    return np.stack([real, imag]).astype(jnp.bfloat16)


def edge(step, length):
    if step < 0:
        return slice(0, RIM)
    if step > 0:
        return slice(length - RIM, length)
    return slice(0, length)


def zone(step):
    return (slice(0, RIM), slice(RIM, RIM + TILE), slice(RIM + TILE, 2 * RIM + TILE))[step + 1]


def shape_of(planes, side):
    return (planes, TILE if side[0] == 0 else RIM, TILE if side[1] == 0 else RIM)


def inside(row, col):
    rows, cols = lax.axis_size("row"), lax.axis_size("col")
    return (row >= 0) & (row < rows) & (col >= 0) & (col < cols)


def exchange(sources, landings, sends, receives):
    row, col = lax.axis_index("row"), lax.axis_index("col")
    barrier = pltpu.get_barrier_semaphore()
    for down, right in SIDES:

        @pl.when(inside(row + down, col + right))
        def _():
            pl.semaphore_signal(
                barrier,
                inc=1,
                device_id=(row + down, col + right),
                device_id_type=pl.DeviceIdType.MESH,
            )

    peers = 0
    for down, right in SIDES:
        peers = peers + jnp.where(inside(row + down, col + right), 1, 0)
    pl.semaphore_wait(barrier, peers)

    def copy_of(i, down, right):
        return pltpu.make_async_remote_copy(
            src_ref=sources[i],
            dst_ref=landings[i],
            send_sem=sends.at[i],
            recv_sem=receives.at[i],
            device_id=(row + down, col + right),
            device_id_type=pl.DeviceIdType.MESH,
        )

    for i in (4, 5, 6, 7, 0, 1, 2, 3):
        down, right = SIDES[i]

        @pl.when(inside(row + down, col + right))
        def _():
            copy_of(i, down, right).start()

    for i, (down, right) in enumerate(SIDES):
        has_source = inside(row - down, col - right)

        @pl.when(jnp.logical_not(has_source))
        def _():
            landings[i][...] = jnp.zeros(landings[i].shape, jnp.float32)

    for i, (down, right) in enumerate(SIDES):

        @pl.when(inside(row - down, col - right))
        def _():
            copy_of(i, -down, -right).wait_recv()

    for i, (down, right) in enumerate(SIDES):

        @pl.when(inside(row + down, col + right))
        def _():
            copy_of(i, down, right).wait_send()


def halo_kernel(field_ref, *refs):
    sources = [
        field_ref.at[:, edge(side[0], TILE), edge(side[1], TILE)] for side in SIDES
    ]
    exchange(sources, refs[:8], refs[8], refs[9])


def gradient_kernel(
    planes, offs, cnt, own, *refs
):
    halos = refs[:8]
    probe, amps, table = refs[8:11]
    center_out = refs[11]
    outs = refs[12:20]
    ext, canvas, left_m, right_m, wave, half, full = refs[20:]

    real, imag = table[0], table[1]
    left_m[:TILE, :TILE] = real
    left_m[:TILE, TILE:] = -imag
    left_m[TILE:, :TILE] = imag
    left_m[TILE:, TILE:] = real
    right_m[:TILE, :TILE] = real
    right_m[:TILE, TILE:] = imag
    right_m[TILE:, :TILE] = -imag
    right_m[TILE:, TILE:] = real

    canvas[...] = jnp.zeros_like(canvas)
    ext[:, 4] = jnp.zeros_like(ext[:, 4])
    for block in range(2):
        ext[:, 1 + block, RIM : RIM + TILE, :] = own[:, :, block * LANES : (block + 1) * LANES]
    for (down, right), halo in zip(SIDES, halos):
        rows = zone(-down)
        if right == 0:
            ext[:, 1, rows, :] = halo[:, :, :LANES]
            ext[:, 2, rows, :] = halo[:, :, LANES:]
        else:
            ext[:, 3 if right < 0 else 0, rows, :] = halo[...]

    lane = lax.broadcasted_iota(jnp.int32, (CHUNK, LANES), 1)

    def one_slot(slot, carry):
        top = offs[slot, 0]
        left = offs[slot, 1]
        first = left // LANES
        shift = left % LANES
        back = (LANES - shift) % LANES
        keep = lane < LANES - shift
        late = lane >= shift
        for at in range(0, TILE, CHUNK):
            rows = pl.ds(top + at, CHUNK)
            parts = []
            for p in range(2):
                rolled = [
                    pltpu.roll(ext[p, first + b, rows, :], back, 1) for b in range(3)
                ]
                parts.append([jnp.where(keep, rolled[b], rolled[b + 1]) for b in range(2)])
            for b in range(2):
                cols = slice(b * LANES, (b + 1) * LANES)
                pr = probe[0, at : at + CHUNK, cols]
                pi = probe[1, at : at + CHUNK, cols]
                wr, wi = parts[0][b], parts[1][b]
                wave[at : at + CHUNK, cols] = (pr * wr - pi * wi).astype(jnp.bfloat16)
                wave[TILE + at : TILE + at + CHUNK, cols] = (pr * wi + pi * wr).astype(jnp.bfloat16)

        def by_rows(matrix):
            product = jnp.dot(matrix[...], wave[...], preferred_element_type=jnp.float32)
            half[:, :TILE] = product[:TILE].astype(jnp.bfloat16)
            half[:, TILE:] = product[TILE:].astype(jnp.bfloat16)

        def by_cols(matrix):
            full[...] = jnp.dot(half[...], matrix[...], preferred_element_type=jnp.float32)

        by_rows(left_m)
        by_cols(right_m)
        for at in range(0, TILE, CHUNK):
            sr = full[at : at + CHUNK, :TILE]
            si = full[at : at + CHUNK, TILE:]
            amp = amps[slot, at : at + CHUNK, :].astype(jnp.float32)
            factor = 1.0 - amp * lax.rsqrt(sr * sr + si * si + smooth_term)
            wave[at : at + CHUNK, :] = (sr * factor).astype(jnp.bfloat16)
            wave[TILE + at : TILE + at + CHUNK, :] = (si * factor).astype(jnp.bfloat16)
        by_rows(right_m)
        by_cols(left_m)
        for at in range(0, TILE, CHUNK):
            rows = pl.ds(top + at, CHUNK)
            pieces = [[] for _ in range(planes)]
            for b in range(2):
                cols = slice(b * LANES, (b + 1) * LANES)
                pr = probe[0, at : at + CHUNK, cols]
                pi = probe[1, at : at + CHUNK, cols]
                br = full[at : at + CHUNK, cols]
                bi = full[at : at + CHUNK, TILE + b * LANES : TILE + (b + 1) * LANES]
                pieces[0].append(pltpu.roll(pr * br + pi * bi, shift, 1))
                pieces[1].append(pltpu.roll(pr * bi - pi * br, shift, 1))
                if planes > 2:
                    pieces[2].append(pltpu.roll(pr * pr + pi * pi, shift, 1))
            for p in range(planes):
                a, b = pieces[p]
                canvas[p, first, rows, :] += jnp.where(late, a, 0.0)
                canvas[p, first + 1, rows, :] += jnp.where(late, b, a)
                canvas[p, first + 2, rows, :] += jnp.where(late, 0.0, b)
        return carry

    lax.fori_loop(0, cnt[0], one_slot, 0)

    center_out[:, :, :LANES] = canvas[:, 1, RIM : RIM + TILE, :]
    center_out[:, :, LANES:] = canvas[:, 2, RIM : RIM + TILE, :]
    for (down, right), out in zip(SIDES, outs):
        rows = zone(down)
        if right == 0:
            out[:, :, :LANES] = canvas[:, 1, rows, :]
            out[:, :, LANES:] = canvas[:, 2, rows, :]
        else:
            out[...] = canvas[:, 0 if right < 0 else 3, rows, :]


def update_kernel(first, own, center, *refs):
    pieces = refs[:8]
    refs = refs[8:]
    if not first:
        scale_in = refs[0]
        refs = refs[1:]
    new = refs[0]
    landed = refs[-11:-3]
    total, sends, receives = refs[-3:]
    exchange(pieces, landed, sends, receives)
    total[...] = center[...]
    for (down, right), piece in zip(SIDES, landed):
        total[:, edge(-down, TILE), edge(-right, TILE)] += piece[...]
    if first:
        scale = step_size / (total[2] + regular_term)
        refs[1][...] = scale
    else:
        scale = scale_in[...]
    for p in range(2):
        new[p] = own[p] - total[p] * scale


def vmem(count):
    return [pl.BlockSpec(memory_space=pltpu.VMEM)] * count


def dma_sems():
    return [pltpu.SemaphoreType.DMA((8,))] * 2


def f32(shape):
    return jax.ShapeDtypeStruct(shape, jnp.float32)


def per_device(object_field, probe_field, amplitudes, offsets, counts):
    table = jnp.asarray(dft_tables())
    offs = offsets.reshape(MAXPOS, 2)
    cnt = counts.reshape(1)
    amps = amplitudes.reshape(MAXPOS, TILE, TILE)
    field = object_field
    edge_shapes = [f32(shape_of(2, side)) for side in SIDES]
    scale = None
    for iteration in range(ITERS):
        first = iteration == 0
        planes = 3 if first else 2
        halos = pl.pallas_call(
            halo_kernel,
            out_shape=edge_shapes,
            in_specs=vmem(1),
            out_specs=vmem(8),
            scratch_shapes=dma_sems(),
            compiler_params=pltpu.CompilerParams(collective_id=0, has_side_effects=True),
            name="halo",
        )(field)
        center, *pieces = pl.pallas_call(
            functools.partial(gradient_kernel, planes),
            out_shape=[f32((planes, TILE, TILE))] + [f32(shape_of(planes, s)) for s in SIDES],
            in_specs=[pl.BlockSpec(memory_space=pltpu.SMEM)] * 2 + vmem(12),
            out_specs=vmem(9),
            scratch_shapes=[
                pltpu.VMEM((2, 5, 2 * TILE, LANES), jnp.float32),
                pltpu.VMEM((planes, 5, 2 * TILE, LANES), jnp.float32),
                pltpu.VMEM((2 * TILE, 2 * TILE), jnp.bfloat16),
                pltpu.VMEM((2 * TILE, 2 * TILE), jnp.bfloat16),
                pltpu.VMEM((2 * TILE, TILE), jnp.bfloat16),
                pltpu.VMEM((TILE, 2 * TILE), jnp.bfloat16),
                pltpu.VMEM((TILE, 2 * TILE), jnp.float32),
            ],
            name=f"gradient{iteration}",
        )(offs, cnt, field, *halos, probe_field, amps, table)
        operands = [field, center, *pieces] + ([] if first else [scale])
        shapes = [f32((2, TILE, TILE))]
        if first:
            shapes.append(f32((TILE, TILE)))
        results = pl.pallas_call(
            functools.partial(update_kernel, first),
            out_shape=shapes,
            in_specs=vmem(len(operands)),
            out_specs=vmem(len(shapes)),
            scratch_shapes=[pltpu.VMEM(shape_of(planes, s), jnp.float32) for s in SIDES]
            + [pltpu.VMEM((planes, TILE, TILE), jnp.float32)]
            + dma_sems(),
            compiler_params=pltpu.CompilerParams(
                collective_id=1 + iteration, has_side_effects=True
            ),
            name=f"update{iteration}",
        )(*operands)
        field = results[0]
        if first:
            scale = results[1]
    return field


def solution(mesh):
    in_specs = (
        P(None, "row", "col"),
        P(),
        P("row", "col", None, None, None),
        P("row", "col", None, None),
        P("row", "col"),
    )
    out_specs = P(None, "row", "col")
    return jax.shard_map(
        per_device, mesh=mesh, in_specs=in_specs, out_specs=out_specs, check_vma=False
    )
```

profile of v0, /device:TPU:9, one launch (start us, length us, event | category | flops | bytes accessed | tf_op | source)
XLA Modules:
  0.0 108.4 jit_solution(1084772617164432690)
XLA Ops:
  0.7 0.0 copy-start
  0.7 0.7 copy-done
  1.3 0.7 copy.7.offs
  2.0 17.6 %halo.2 = (f32[2,128,256]{2,1,0:T(8,128)}, f32[2,128,256]{2,1,0:T(8,128)}, f32[2,256,128]{2,1,0:T(8,128)}, f32[2,256,128]{2,1,0:T(8,128)}, f32[2,128,128]{2,1,0:...) custom-call(f32[2,256,256]{2,1,0:T(8,128)} %own.3), custom_call_target="tpu_custom_call" | custom-call | tf_op jit(solution)/shard_map/halo/pallas_call | solution.py:275
  19.6 13.2 %gradient0.1 = (f32[3,256,256]{2,1,0:T(8,128)}, f32[3,128,256]{2,1,0:T(8,128)}, f32[3,128,256]{2,1,0:T(8,128)}, f32[3,256,128]{2,1,0:T(8,128)}, f32[3,256,128]{2...) custom-call(s32[6,2]{1,0:T(8,128)} %copy.7.offs, ...), custom_call_target="tpu_custom_call" | custom-call | tf_op jit(solution)/shard_map/gradient0/pallas_call | solution.py:284
  32.8 25.0 %update0.1 = (f32[2,256,256]{2,1,0:T(8,128)}, f32[256,256]{1,0:T(8,128)}) custom-call(f32[2,256,256]{2,1,0:T(8,128)} %own.3, f32[3,256,256]{2,1,0:T(8,128)} %get-tuple-element.49.center, f32[3,128,256]{2,1,0:T(8,128)} %get-tuple-element.50.refs_0_, f32[3,128,256]{2,1,0:T(8,128)} %get-tuple-element.51.refs_1_, f32[3,256,128]{2,1,0:T(8,128)} %get-tuple-element.52.refs_2_, ...), custom_call_target="tpu_custom_call" | custom-call | tf_op jit(solution)/shard_map/update0/pallas_call | solution.py:304
  57.8 16.1 %halo.3 = (f32[2,128,256]{2,1,0:T(8,128)}, f32[2,128,256]{2,1,0:T(8,128)}, f32[2,256,128]{2,1,0:T(8,128)}, f32[2,256,128]{2,1,0:T(8,128)}, f32[2,128,128]{2,1,0:...) custom-call(f32[2,256,256]{2,1,0:T(8,128)} %get-tuple-element.58.field_ref.own), custom_call_target="tpu_custom_call" | custom-call | tf_op jit(solution)/shard_map/halo/pallas_call | solution.py:275
  74.0 12.7 %gradient1.1 = (f32[2,256,256]{2,1,0:T(8,128)}, f32[2,128,256]{2,1,0:T(8,128)}, f32[2,128,256]{2,1,0:T(8,128)}, f32[2,256,128]{2,1,0:T(8,128)}, f32[2,256,128]{2...) custom-call(s32[6,2]{1,0:T(8,128)} %copy.7.offs, ...), custom_call_target="tpu_custom_call" | custom-call | tf_op jit(solution)/shard_map/gradient1/pallas_call | solution.py:284
  86.7 19.8 %update1.1 = f32[2,256,256]{2,1,0:T(8,128)} custom-call(f32[2,256,256]{2,1,0:T(8,128)} %get-tuple-element.58.field_ref.own, f32[2,256,256]{2,1,0:T(8,128)} %get-tuple-element.67.center, f32[2,128,256]{2,1,0:T(8,128)} %get-tuple-element.68.refs_0_, f32[2,128,256]{2,1,0:T(8,128)} %get-tuple-element.69.refs_1_, f32[2,256,128]{2,1,0:T(8,128)} %get-tuple-element.70.refs_2_, ...), custom_call_target="tpu_custom_call" | custom-call | tf_op jit(solution)/shard_map/update1/pallas_call | solution.py:304
  106.5 1.9 %copy.11 = f32[2,256,256]{2,1,0:T(8,128)} copy(f32[2,256,256]{2,1,0:T(8,128)} %update1.1) | data formatting | bytes 1048576
Async XLA Ops:
  0.7 0.7 copy-start
where the time goes:
time: 108 us
  Pallas kernels  104 us (96%)
  local copies, waits for them, and re-layouts  3.22 us (3%)
    pallas_call x2, Pallas kernels, per_device(): pl.pallas_call(functools.partial(update_kernel, first), out_shape=shapes,...  44.8 us
    pallas_call x2, Pallas kernels, per_device(): pl.pallas_call(halo_kernel, out_shape=edge_shapes, in_specs=vmem(1), out_...  33.8 us
    pallas_call x2, Pallas kernels, per_device(): pl.pallas_call(functools.partial(gradient_kernel, planes), out_shape=[f32...  25.9 us
    unnamed x3, local copies, waits for them, and re-layouts  2.54 us

commit v1 on v0

--- a/solution.py
+++ b/solution.py
@@ -15,6 +15,7 @@
 ITERS = 2
 LANES = 128
 CHUNK = 64
+VMEM_LIMIT = 28 * 1024 * 1024
 
 smooth_term = 0.25
 step_size = 0.5
@@ -55,12 +56,14 @@
     return (row >= 0) & (row < rows) & (col >= 0) & (col < cols)
 
 
-def exchange(sources, landings, sends, receives):
-    row, col = lax.axis_index("row"), lax.axis_index("col")
+def greet(row, col):
     barrier = pltpu.get_barrier_semaphore()
-    for down, right in SIDES:
-
-        @pl.when(inside(row + down, col + right))
+    peers = 0
+    for down, right in SIDES[:4]:
+        present = inside(row + down, col + right)
+        peers = peers + jnp.where(present, 1, 0)
+
+        @pl.when(present)
         def _():
             pl.semaphore_signal(
                 barrier,
@@ -69,53 +72,114 @@
                 device_id_type=pl.DeviceIdType.MESH,
             )
 
-    peers = 0
-    for down, right in SIDES:
-        peers = peers + jnp.where(inside(row + down, col + right), 1, 0)
     pl.semaphore_wait(barrier, peers)
 
-    def copy_of(i, down, right):
-        return pltpu.make_async_remote_copy(
-            src_ref=sources[i],
-            dst_ref=landings[i],
-            send_sem=sends.at[i],
-            recv_sem=receives.at[i],
-            device_id=(row + down, col + right),
-            device_id_type=pl.DeviceIdType.MESH,
+
+def transfer(source, landing, sends, receives, slot, device):
+    return pltpu.make_async_remote_copy(
+        src_ref=source,
+        dst_ref=landing,
+        send_sem=sends.at[slot],
+        recv_sem=receives.at[slot],
+        device_id=device,
+        device_id_type=pl.DeviceIdType.MESH,
+    )
+
+
+def half_of(right):
+    return slice(0, LANES) if right < 0 else slice(LANES, 2 * LANES)
+
+
+def half_slot(down, right):
+    return (0 if down < 0 else 1) + (0 if right < 0 else 8)
+
+
+CORNERS = SIDES[4:]
+
+
+def halo_kernel(field, *refs):
+    outs = refs[:8]
+    sends, receives = refs[8:]
+    row, col = lax.axis_index("row"), lax.axis_index("col")
+    greet(row, col)
+
+    def row_copy(down, right, device):
+        half = half_of(right)
+        return transfer(
+            field.at[:, edge(down, TILE), half],
+            outs[SIDES.index((down, 0))].at[:, :, half],
+            sends,
+            receives,
+            half_slot(down, right),
+            device,
         )
 
-    for i in (4, 5, 6, 7, 0, 1, 2, 3):
-        down, right = SIDES[i]
-
-        @pl.when(inside(row + down, col + right))
-        def _():
-            copy_of(i, down, right).start()
-
-    for i, (down, right) in enumerate(SIDES):
-        has_source = inside(row - down, col - right)
-
-        @pl.when(jnp.logical_not(has_source))
-        def _():
-            landings[i][...] = jnp.zeros(landings[i].shape, jnp.float32)
-
-    for i, (down, right) in enumerate(SIDES):
+    def col_copy(right, device):
+        at = SIDES.index((0, right))
+        return transfer(
+            field.at[:, :, edge(right, TILE)], outs[at], sends, receives, at, device
+        )
+
+    def corner_copy(down, right, device):
+        at = SIDES.index((down, right))
+        landed = outs[SIDES.index((down, 0))].at[:, :, half_of(right)]
+        return transfer(landed, outs[at], sends, receives, at, device)
+
+    for down, right in CORNERS:
+
+        @pl.when(inside(row + down, col))
+        def _():
+            row_copy(down, right, (row + down, col)).start()
+
+    for right in (-1, 1):
+
+        @pl.when(inside(row, col + right))
+        def _():
+            col_copy(right, (row, col + right)).start()
+
+    for (down, right), out in zip(SIDES, outs):
+
+        @pl.when(jnp.logical_not(inside(row - down, col - right)))
+        def _():
+            out[...] = jnp.zeros(out.shape, jnp.float32)
+
+    for down, right in CORNERS:
+
+        @pl.when(inside(row - down, col))
+        def _():
+            row_copy(down, right, (row - down, col)).wait_recv()
+
+        @pl.when(inside(row - down, col) & inside(row, col + right))
+        def _():
+            corner_copy(down, right, (row, col + right)).start()
+
+    for right in (-1, 1):
+
+        @pl.when(inside(row, col - right))
+        def _():
+            col_copy(right, (row, col - right)).wait_recv()
+
+    for down, right in CORNERS:
 
         @pl.when(inside(row - down, col - right))
         def _():
-            copy_of(i, -down, -right).wait_recv()
-
-    for i, (down, right) in enumerate(SIDES):
-
-        @pl.when(inside(row + down, col + right))
-        def _():
-            copy_of(i, down, right).wait_send()
-
-
-def halo_kernel(field_ref, *refs):
-    sources = [
-        field_ref.at[:, edge(side[0], TILE), edge(side[1], TILE)] for side in SIDES
-    ]
-    exchange(sources, refs[:8], refs[8], refs[9])
+            corner_copy(down, right, (row, col - right)).wait_recv()
+
+    for down, right in CORNERS:
+
+        @pl.when(inside(row + down, col))
+        def _():
+            row_copy(down, right, (row + down, col)).wait_send()
+
+        @pl.when(inside(row - down, col) & inside(row, col + right))
+        def _():
+            corner_copy(down, right, (row, col + right)).wait_send()
+
+    for right in (-1, 1):
+
+        @pl.when(inside(row, col + right))
+        def _():
+            col_copy(right, (row, col + right)).wait_send()
 
 
 def gradient_kernel(
@@ -234,12 +298,100 @@
         scale_in = refs[0]
         refs = refs[1:]
     new = refs[0]
-    landed = refs[-11:-3]
+    landed = refs[-13:-5]
+    sums = refs[-5:-3]
     total, sends, receives = refs[-3:]
-    exchange(pieces, landed, sends, receives)
+    row, col = lax.axis_index("row"), lax.axis_index("col")
+    greet(row, col)
+
+    def corner_copy(down, right, device):
+        at = SIDES.index((down, right))
+        return transfer(pieces[at], landed[at], sends, receives, at, device)
+
+    def col_copy(right, device):
+        at = SIDES.index((0, right))
+        return transfer(pieces[at], landed[at], sends, receives, at, device)
+
+    def row_copy(down, right, device):
+        at = SIDES.index((down, 0))
+        half = half_of(right)
+        return transfer(
+            sums[at].at[:, :, half],
+            landed[at].at[:, :, half],
+            sends,
+            receives,
+            half_slot(down, right),
+            device,
+        )
+
+    for down, right in CORNERS:
+
+        @pl.when(inside(row + down, col + right))
+        def _():
+            corner_copy(down, right, (row, col + right)).start()
+
+    for right in (-1, 1):
+
+        @pl.when(inside(row, col + right))
+        def _():
+            col_copy(right, (row, col + right)).start()
+
+    for at, (down, right) in enumerate(SIDES[:4]):
+
+        @pl.when(jnp.logical_not(inside(row - down, col - right)))
+        def _():
+            landed[at][...] = jnp.zeros(landed[at].shape, jnp.float32)
+
+    for at in range(2):
+        sums[at][...] = pieces[at][...]
+    for down, right in CORNERS:
+
+        @pl.when(inside(row + down, col) & inside(row, col - right))
+        def _():
+            corner_copy(down, right, (row, col - right)).wait_recv()
+            at = SIDES.index((down, 0))
+            sums[at][:, :, half_of(-right)] += landed[SIDES.index((down, right))][...]
+
     total[...] = center[...]
-    for (down, right), piece in zip(SIDES, landed):
-        total[:, edge(-down, TILE), edge(-right, TILE)] += piece[...]
+    for down, right in CORNERS:
+
+        @pl.when(inside(row + down, col))
+        def _():
+            row_copy(down, right, (row + down, col)).start()
+
+    for right in (-1, 1):
+
+        @pl.when(inside(row, col - right))
+        def _():
+            col_copy(right, (row, col - right)).wait_recv()
+
+        total[:, :, edge(-right, TILE)] += landed[SIDES.index((0, right))][...]
+
+    for down, right in CORNERS:
+
+        @pl.when(inside(row - down, col))
+        def _():
+            row_copy(down, right, (row - down, col)).wait_recv()
+
+    for down in (-1, 1):
+        total[:, edge(-down, TILE), :] += landed[SIDES.index((down, 0))][...]
+
+    for down, right in CORNERS:
+
+        @pl.when(inside(row + down, col + right))
+        def _():
+            corner_copy(down, right, (row, col + right)).wait_send()
+
+        @pl.when(inside(row + down, col))
+        def _():
+            row_copy(down, right, (row + down, col)).wait_send()
+
+    for right in (-1, 1):
+
+        @pl.when(inside(row, col + right))
+        def _():
+            col_copy(right, (row, col + right)).wait_send()
+
     if first:
         scale = step_size / (total[2] + regular_term)
         refs[1][...] = scale
@@ -254,7 +406,7 @@
 
 
 def dma_sems():
-    return [pltpu.SemaphoreType.DMA((8,))] * 2
+    return [pltpu.SemaphoreType.DMA((10,))] * 2
 
 
 def f32(shape):
@@ -278,7 +430,7 @@
             in_specs=vmem(1),
             out_specs=vmem(8),
             scratch_shapes=dma_sems(),
-            compiler_params=pltpu.CompilerParams(collective_id=0, has_side_effects=True),
+            compiler_params=pltpu.CompilerParams(collective_id=0, has_side_effects=True, vmem_limit_bytes=VMEM_LIMIT),
             name="halo",
         )(field)
         center, *pieces = pl.pallas_call(
@@ -295,6 +447,7 @@
                 pltpu.VMEM((TILE, 2 * TILE), jnp.bfloat16),
                 pltpu.VMEM((TILE, 2 * TILE), jnp.float32),
             ],
+            compiler_params=pltpu.CompilerParams(vmem_limit_bytes=VMEM_LIMIT),
             name=f"gradient{iteration}",
         )(offs, cnt, field, *halos, probe_field, amps, table)
         operands = [field, center, *pieces] + ([] if first else [scale])
@@ -307,10 +460,13 @@
             in_specs=vmem(len(operands)),
             out_specs=vmem(len(shapes)),
             scratch_shapes=[pltpu.VMEM(shape_of(planes, s), jnp.float32) for s in SIDES]
+            + [pltpu.VMEM((planes, RIM, TILE), jnp.float32)] * 2
             + [pltpu.VMEM((planes, TILE, TILE), jnp.float32)]
             + dma_sems(),
             compiler_params=pltpu.CompilerParams(
-                collective_id=1 + iteration, has_side_effects=True
+                collective_id=1 + iteration,
+                has_side_effects=True,
+                vmem_limit_bytes=VMEM_LIMIT,
             ),
             name=f"update{iteration}",
         )(*operands)

time: 108 us -> 84.8 us (0.79)
  the two profiles are of different devices: /device:TPU:9 before, /device:TPU:18 now
where the time goes in v1:
time: 84.8 us; the launch traced here: 84.1 us
  Pallas kernels  78.6 us (93%)
  local copies, waits for them, and re-layouts  4.7 us (6%)
    pallas_call x2, Pallas kernels, per_device(): pl.pallas_call(functools.partial(update_kernel, first), out_shape=shapes,...  30.1 us
    pallas_call x2, Pallas kernels, per_device(): pl.pallas_call(halo_kernel, out_shape=edge_shapes, in_specs=vmem(1), out_...  24.5 us
    pallas_call x2, Pallas kernels, per_device(): pl.pallas_call(functools.partial(gradient_kernel, planes), out_shape=[f32...  24 us
    unnamed x15, local copies, waits for them, and re-layouts  4.6 us

profile of v1, /device:TPU:18, one launch (start us, length us, event | category | flops | bytes accessed | tf_op | source)
XLA Modules:
  0.0 84.1 jit_solution(11103786184871899373)
XLA Ops:
  0.7 0.0 copy-start.6
  0.7 0.7 copy-done.6
  1.3 0.1 copy.7.offs
  1.4 0.0 copy-start
  1.4 1.0 %copy-done = f32[2,256,256]{2,1,0:T(8,128)S(1)} copy-done((f32[2,256,256]{2,1,0:T(8,128)S(1)}, f32[2,256,256]{2,1,0:T(8,128)}, u32[]{:S(2)}) %copy-start) | copy-done | bytes 524312
  2.5 0.0 copy-start.3
  2.5 12.7 %halo.2 = (f32[2,128,256]{2,1,0:T(8,128)S(1)}, f32[2,128,256]{2,1,0:T(8,128)S(1)}, f32[2,256,128]{2,1,0:T(8,128)S(1)}, f32[2,256,128]{2,1,0:T(8,128)S(1)}, f32[2...) custom-call(f32[2,256,256]{2,1,0:T(8,128)S(1)} %copy-done), custom_call_target="tpu_custom_call" | custom-call | tf_op jit(solution)/shard_map/halo/pallas_call | solution.py:427
  15.1 0.0 copy-done.3
  15.1 0.0 copy-start.1
  15.2 1.1 %copy-done.1 = bf16[1,1,6,256,256]{4,3,2,1,0:T(8,128)(2,1)S(1)} copy-done((bf16[1,1,6,256,256]{4,3,2,1,0:T(8,128)(2,1)S(1)}, bf16[1,1,6,256,256]{4,3,2,1,0:T(8,128)(2,1)}, u32[]{:S(2)}) %copy-start.1) | copy-done | bytes 786456
  16.3 0.0 copy-start.4
  16.3 0.9 %copy-done.4 = bf16[2,256,256]{2,1,0:T(8,128)(2,1)S(1)} copy-done((bf16[2,256,256]{2,1,0:T(8,128)(2,1)S(1)}, bf16[2,256,256]{2,1,0:T(8,128)(2,1)}, u32[]{:S(2)}) %copy-start.4) | copy-done | bytes 262168
  17.2 12.1 %gradient0.1 = (f32[3,256,256]{2,1,0:T(8,128)S(1)}, f32[3,128,256]{2,1,0:T(8,128)S(1)}, f32[3,128,256]{2,1,0:T(8,128)S(1)}, f32[3,256,128]{2,1,0:T(8,128)S(1)}, ...) custom-call(s32[6,2]{1,0:T(8,128)S(1)} %copy.7.offs, ...), custom_call_target="tpu_custom_call" | custom-call | tf_op jit(solution)/shard_map/gradient0/pallas_call | solution.py:436
  29.3 0.0 copy-start.2
  29.3 17.2 %update0.1 = (f32[2,256,256]{2,1,0:T(8,128)S(1)}, f32[256,256]{1,0:T(8,128)S(1)}) custom-call(f32[2,256,256]{2,1,0:T(8,128)S(1)} %copy-done, f32[3,256,256]{2,1,0:T(8,128)S(1)} %get-tuple-element.49.center, f32[3,128,256]{2,1,0:T(8,128)S(1)} %get-tuple-element.50.refs_0_, f32[3,128,256]{2,1,0:T(8,128)S(1)} %get-tuple-element.51.refs_1_, ...), custom_call_target="tpu_custom_call" | custom-call | tf_op jit(solution)/shard_map/update0/pallas_call | solution.py:457
  46.5 0.0 copy-start.5
  46.5 11.9 %halo.3 = (f32[2,128,256]{2,1,0:T(8,128)S(1)}, f32[2,128,256]{2,1,0:T(8,128)S(1)}, f32[2,256,128]{2,1,0:T(8,128)S(1)}, f32[2,256,128]{2,1,0:T(8,128)S(1)}, f32[2...) custom-call(f32[2,256,256]{2,1,0:T(8,128)S(1)} %get-tuple-element.58, ...), custom_call_target="tpu_custom_call" | custom-call | tf_op jit(solution)/shard_map/halo/pallas_call | solution.py:427
  58.4 0.0 copy-done.2
  58.4 0.0 copy-done.5
  58.4 11.9 %gradient1.1 = (f32[2,256,256]{2,1,0:T(8,128)S(1)}, f32[2,128,256]{2,1,0:T(8,128)S(1)}, f32[2,128,256]{2,1,0:T(8,128)S(1)}, f32[2,256,128]{2,1,0:T(8,128)S(1)}, ...) custom-call(s32[6,2]{1,0:T(8,128)S(1)} %copy.7.offs, ...), custom_call_target="tpu_custom_call" | custom-call | tf_op jit(solution)/shard_map/gradient1/pallas_call | solution.py:436
  70.4 12.9 %update1.1 = f32[2,256,256]{2,1,0:T(8,128)S(1)} custom-call(f32[2,256,256]{2,1,0:T(8,128)S(1)} %get-tuple-element.58.field.own, f32[2,256,256]{2,1,0:T(8,128)S(1)} %get-tuple-element.67.center, f32[2,128,256]{2,1,0:T(8,128)S(1)} %get-tuple-element.68.refs_0_, f32[2,128,256]{2,1,0:T(8,128)S(1)} %get-tuple-element.69.refs_1_, ...), custom_call_target="tpu_custom_call" | custom-call | tf_op jit(solution)/shard_map/update1/pallas_call | solution.py:457
  83.3 0.8 copy.11
Async XLA Ops:
  0.7 0.7 copy-start.6
  1.4 1.0 %copy-start = (f32[2,256,256]{2,1,0:T(8,128)S(1)}, f32[2,256,256]{2,1,0:T(8,128)}, u32[]{:S(2)}) copy-start(f32[2,256,256]{2,1,0:T(8,128)} %own.3) | copy-start | bytes 1572868
  2.5 12.7 %copy-start.3 = (f32[2,256,256]{2,1,0:T(8,128)S(1)}, f32[2,256,256]{2,1,0:T(8,128)}, u32[]{:S(2)}) copy-start(f32[2,256,256]{2,1,0:T(8,128)} %refs_8_.3) | copy-start | bytes 1572868
  15.1 1.1 %copy-start.1 = (bf16[1,1,6,256,256]{4,3,2,1,0:T(8,128)(2,1)S(1)}, bf16[1,1,6,256,256]{4,3,2,1,0:T(8,128)(2,1)}, u32[]{:S(2)}) copy-start(bf16[1,1,6,256,256]{4,3,2,1,0:T(8,128)(2,1)} %param.8) | copy-start | bytes 2359300
  16.3 0.9 %copy-start.4 = (bf16[2,256,256]{2,1,0:T(8,128)(2,1)S(1)}, bf16[2,256,256]{2,1,0:T(8,128)(2,1)}, u32[]{:S(2)}) copy-start(bf16[2,256,256]{2,1,0:T(8,128)(2,1)} %constant.2.clone.refs_10_) | copy-start | bytes 786436
  29.3 29.1 %copy-start.2 = (bf16[1,1,6,256,256]{4,3,2,1,0:T(8,128)(2,1)S(1)}, bf16[1,1,6,256,256]{4,3,2,1,0:T(8,128)(2,1)}, u32[]{:S(2)}) copy-start(bf16[1,1,6,256,256]{4,3,2,1,0:T(8,128)(2,1)} %param.8) | copy-start | bytes 2359300
  46.5 11.9 %copy-start.5 = (bf16[2,256,256]{2,1,0:T(8,128)(2,1)S(1)}, bf16[2,256,256]{2,1,0:T(8,128)(2,1)}, u32[]{:S(2)}) copy-start(bf16[2,256,256]{2,1,0:T(8,128)(2,1)} %constant.2.clone.refs_10_) | copy-start | bytes 786436
